TPU v7x, 32 devices: a whole 2x2x4 slice. The times are simulated.
32 devices in a mesh: row: 8 (over z, core), col: 4 (over y, x).
Axes of the slice: x: 2, y: 2, z: 4, core: 2. Of those that a mesh axis runs over, the one named last changes fastest.
Arguments:
- matrix: bfloat16 [12288, 12288], P('row', 'col'), may hold values from -8 to 8, as said below
- panels: bfloat16 [2, 12288, 128], P(None, 'row'), may hold values from -1 to 1
Outputs:
- updated: bfloat16 [12288, 12288], P('row', 'col')
Inputs may be any that keep to these rules, and one draw needn't show every extreme that they name: matrix is exactly symmetric.
All inputs are finite; a program needn't handle non-finite values.
Results may differ from a plain program's by a relative error of at most 0.015.
Values may be sent and summed in bfloat16 or wider, within the bound.
No kernel may reach another device: no remote copies, remote signals or barrier semaphores. Data moves between devices by JAX's collectives and lax.ppermute only.
A program may use at most 128 MiB of HBM per device.

v0:
```python
import jax
import jax.numpy as jnp
from jax import lax
from jax.sharding import PartitionSpec as P

PANELS = 2


def spread(block, axis, source):
    block = jnp.where(lax.axis_index(axis) == source, block, jnp.zeros_like(block))
    return lax.psum(block, axis)


def per_device(matrix, panels):
    row_count = lax.axis_size("row")
    col_count = lax.axis_size("col")
    owner_ratio = row_count // col_count
    row_index = lax.axis_index("row")
    col_index = lax.axis_index("col")
    a_tile = matrix
    n_rows = a_tile.shape[0]
    n_cols = a_tile.shape[1]
    for panel in range(PANELS):
        v_rows = panels[panel]
        gathered = lax.all_gather(v_rows, "row", axis=0, tiled=True)
        v_cols = lax.dynamic_slice_in_dim(gathered, col_index * n_cols, n_cols, 0)
        tile_now = a_tile
        av_fine = lax.psum_scatter(
            lax.dot_general(
                tile_now, v_rows, (((0,), (0,)), ((), ())), preferred_element_type=jnp.float32
            ),
            "row",
            scatter_dimension=0,
            tiled=True,
        )
        av_cols = lax.all_gather(av_fine, "row", axis=0, tiled=True)
        own_rows = lax.dynamic_slice_in_dim(av_cols, row_index % owner_ratio * n_rows, n_rows, 0)
        av_rows = spread(own_rows, "col", row_index // owner_ratio)
        local_sum = jnp.dot(v_rows.astype(jnp.float32).T, av_rows, precision=lax.Precision.HIGHEST)
        curvature = lax.psum(local_sum.astype(jnp.bfloat16), "row").astype(jnp.float32)
        w_cols = (
            av_cols
            - 0.5 * jnp.dot(v_cols.astype(jnp.float32), curvature, precision=lax.Precision.HIGHEST)
        ).astype(jnp.bfloat16)
        w_rows = (
            av_rows
            - 0.5 * jnp.dot(v_rows.astype(jnp.float32), curvature, precision=lax.Precision.HIGHEST)
        ).astype(jnp.bfloat16)
        update = lax.dot_general(
            v_rows, w_cols, (((1,), (1,)), ((), ())), preferred_element_type=jnp.float32
        )
        update = update + lax.dot_general(
            w_rows, v_cols, (((1,), (1,)), ((), ())), preferred_element_type=jnp.float32
        )
        a_tile = (a_tile.astype(jnp.float32) - update).astype(jnp.bfloat16)
    return a_tile


def solution(mesh):
    in_specs = (P("row", "col"), P(None, "row", None))
    out_specs = P("row", "col")
    return jax.shard_map(
        per_device, mesh=mesh, in_specs=in_specs, out_specs=out_specs, check_vma=False
    )
```

profile of v0, /device:TPU:0, one launch (start us, length us, event | category | flops | bytes accessed | tf_op | source)
XLA Modules:
  0.0 393.4 jit_solution(9624634092060317979)
XLA Ops:
  6.5 7.5 %fusion.34 = f32[3072,128]{1,0:T(8,128)} fusion(bf16[1536,3072]{1,0:T(8,128)(2,1)} %param.2, bf16[2,1536,128]{2,1,0:T(8,128)(2,1)} %param.3), kind=kOutput, calls=%fused_computation.44 | convolution fusion | flops 1207959552 | bytes 11403264 | tf_op jit(solution)/shard_map/dot_general | solution.py:29
  14.1 0.0 all-gather.7.cloned.1.call-start
  14.2 37.0 %reduce-scatter.3.cloned.1.call-done = f32[384,128]{1,0:T(8,128)} async-done(((f32[3072,128]{1,0:T(8,128)}), f32[384,128]{1,0:T(8,128)}) %reduce-scatter.3.cloned.1.call-update) | async-done | bytes 196624 | tf_op jit(solution)/shard_map/reduce_scatter | solution.py:28
  51.2 25.2 %all-gather.7.cloned.1.call-done = f32[3072,128]{1,0:T(8,128)} async-done(((f32[384,128]{1,0:T(8,128)}), f32[3072,128]{1,0:T(8,128)}) %all-gather.7.cloned.1.call-update) | async-done | bytes 1572880 | tf_op jit(solution)/shard_map/all_gather | solution.py:36
  76.4 2.1 dynamic-slice_select_fusion.1
  78.5 0.0 all-gather.11.cloned.1.call-start
  78.5 0.9 fusion.48
  79.5 0.0 reduce-scatter.5.cloned.1.call-start
  79.6 12.8 %copy.3 = bf16[1536,3072]{0,1:T(8,128)(2,1)} copy(bf16[1536,3072]{1,0:T(8,128)(2,1)} %param.2) | data formatting | bytes 18874368 | tf_op args[0]
  92.3 34.9 %all-reduce.3.cloned.1.call-done = f32[1536,128]{1,0:T(8,128)} async-done(((f32[1536,128]{1,0:T(8,128)}), f32[1536,128]{1,0:T(8,128)}) %all-reduce.3.cloned.1.call-update) | async-done | bytes 786448 | tf_op jit(solution)/shard_map/psum | solution.py:11
  127.3 1.9 fusion.14
  129.2 29.9 %psum.29 = bf16[128,128]{0,1:T(8,128)(2,1)S(1)} all-reduce(bf16[128,128]{0,1:T(8,128)(2,1)S(1)} %fusion.14), channel_id=1, replica_groups=mesh['row'=8,'col'=4] {'row'}, use_global_device_ids=true, to_apply=%region_2.3 | all-reduce | flops 16384 | bytes 65536 | tf_op jit(solution)/shard_map/psum | solution.py:40
  159.1 8.3 %all-gather.11.cloned.1.call-done = bf16[1,12288,128]{2,1,0:T(8,128)(2,1)} async-done(((bf16[1,1536,128]{2,1,0:T(8,128)(2,1)}), bf16[1,12288,128]{2,1,0:T(8,128)(2,1)}) %all-gather.11.cloned.1.call-update) | async-done | bytes 3145744 | tf_op jit(solution)/shard_map/all_gather | solution.py:25
  167.4 1.5 fusion.6
  168.9 8.0 %fusion.30 = f32[3072,1536]{1,0:T(8,128)} fusion(bf16[3072,128]{1,0:T(8,128)(2,1)S(1)} %fusion.6, bf16[2,1536,128]{2,1,0:T(8,128)(2,1)S(1)} %copy-done), kind=kOutput, calls=%fused_computation.40 | convolution fusion | flops 1207959552 | bytes 20054016 | tf_op jit(solution)/shard_map/dot_general | solution.py:49
  176.9 0.3 fusion.13
  177.2 14.6 %fusion.3 = bf16[1536,3072]{0,1:T(8,128)(2,1)} fusion(f32[3072,1536]{1,0:T(8,128)} %fusion.30, bf16[1536,3072]{0,1:T(8,128)(2,1)} %copy.3, bf16[1536,128]{1,0:T(8,128)(2,1)S(1)} %fusion.13, bf16[1,12288,128]{2,1,0:T(8,128)(2,1)} %all-gather.11.cloned.1.call-done, s32[]{:T(128)S(6)} %select_n.34), kind=kOutput, calls=%fused_computation.5 | convolution fusion | flops 1226833920 | bytes 38928388 | tf_op jit(solution)/shard_map/dot_general | solution.py:52
  191.8 7.5 %fusion.28 = f32[3072,128]{1,0:T(8,128)} fusion(bf16[1536,3072]{0,1:T(8,128)(2,1)} %fusion.3, bf16[2,1536,128]{2,1,0:T(8,128)(2,1)S(1)} %copy-done), kind=kOutput, calls=%fused_computation.38 | convolution fusion | flops 1207959552 | bytes 11403264 | tf_op jit(solution)/shard_map/dot_general | solution.py:29
  199.3 33.1 %reduce-scatter.5.cloned.1.call-done = f32[384,128]{1,0:T(8,128)} async-done(((f32[3072,128]{1,0:T(8,128)}), f32[384,128]{1,0:T(8,128)}) %reduce-scatter.5.cloned.1.call-update) | async-done | bytes 196624 | tf_op jit(solution)/shard_map/reduce_scatter | solution.py:28
  232.5 25.2 %all-gather.9.cloned.1.call-done = f32[3072,128]{1,0:T(8,128)} async-done(((f32[384,128]{1,0:T(8,128)}), f32[3072,128]{1,0:T(8,128)}) %all-gather.9.cloned.1.call-update) | async-done | bytes 1572880 | tf_op jit(solution)/shard_map/all_gather | solution.py:36
  257.7 2.1 dynamic-slice_select_fusion
  259.8 0.0 all-gather.13.cloned.1.call-start
  259.9 0.7 all-gather.13.cloned.1.call-update
  260.6 48.0 %all-reduce.5.cloned.1.call-done = f32[1536,128]{1,0:T(8,128)} async-done(((f32[1536,128]{1,0:T(8,128)}), f32[1536,128]{1,0:T(8,128)}) %all-reduce.5.cloned.1.call-update) | async-done | bytes 786448 | tf_op jit(solution)/shard_map/psum | solution.py:11
  308.6 1.9 fusion.15
  310.5 30.2 %psum.31 = bf16[128,128]{0,1:T(8,128)(2,1)S(1)} all-reduce(bf16[128,128]{0,1:T(8,128)(2,1)S(1)} %fusion.15), channel_id=1, replica_groups=mesh['row'=8,'col'=4] {'row'}, use_global_device_ids=true, to_apply=%region_5.6 | all-reduce | flops 16384 | bytes 65536 | tf_op jit(solution)/shard_map/psum | solution.py:40
  340.7 8.1 %all-gather.13.cloned.1.call-done = bf16[1,12288,128]{2,1,0:T(8,128)(2,1)} async-done(((bf16[1,1536,128]{2,1,0:T(8,128)(2,1)}), bf16[1,12288,128]{2,1,0:T(8,128)(2,1)}) %all-gather.13.cloned.1.call-update) | async-done | bytes 3145744 | tf_op jit(solution)/shard_map/all_gather | solution.py:25
  348.8 2.0 fusion.7
  350.9 8.0 %fusion.24 = f32[3072,1536]{1,0:T(8,128)} fusion(bf16[3072,128]{1,0:T(8,128)(2,1)S(1)} %fusion.7, bf16[2,1536,128]{2,1,0:T(8,128)(2,1)S(1)} %copy-done), kind=kOutput, calls=%fused_computation.34 | convolution fusion | flops 1207959552 | bytes 20054016 | tf_op jit(solution)/shard_map/dot_general | solution.py:49
  358.9 0.3 fusion.12
  359.1 14.8 %fusion.1 = bf16[1536,3072]{0,1:T(8,128)(2,1)} fusion(f32[3072,1536]{1,0:T(8,128)} %fusion.24, bf16[1536,3072]{0,1:T(8,128)(2,1)} %fusion.3, bf16[1536,128]{1,0:T(8,128)(2,1)S(1)} %fusion.12, bf16[1,12288,128]{2,1,0:T(8,128)(2,1)} %all-gather.13.cloned.1.call-done, s32[]{:T(128)S(6)} %select_n.34), kind=kOutput, calls=%fused_computation.2 | convolution fusion | flops 1226833920 | bytes 38928388 | tf_op jit(solution)/shard_map/dot_general | solution.py:52
  374.0 12.6 %copy.6 = bf16[1536,3072]{1,0:T(8,128)(2,1)} copy(bf16[1536,3072]{0,1:T(8,128)(2,1)} %fusion.1) | data formatting | bytes 18874368 | tf_op jit(solution)/shard_map/convert_element_type | solution.py:55
  (19 shorter events, 0.3 us)
Async XLA Ops:
  6.5 72.0 %copy-start = (bf16[2,1536,128]{2,1,0:T(8,128)(2,1)S(1)}, bf16[2,1536,128]{2,1,0:T(8,128)(2,1)}, u32[]{:S(2)}) copy-start(bf16[2,1536,128]{2,1,0:T(8,128)(2,1)} %param.3) | copy-start | bytes 2359300
  6.5 44.6 %reduce-scatter.3.cloned.1.call-start = ((), (), s32[]{:S(2)}) async-start(), calls=%async_computation.2 | async-start | bytes 1769472 | tf_op jit(solution)/shard_map/reduce_scatter | solution.py:28
  14.1 62.3 %all-gather.7.cloned.1.call-start = ((), (), s32[]{:S(2)}) async-start(), calls=%async_computation.3 | async-start | bytes 1769472 | tf_op jit(solution)/shard_map/all_gather | solution.py:36
  51.2 76.1 %all-reduce.3.cloned.1.call-start = ((), (), s32[]{:S(2)}) async-start(), calls=%async_computation.4 | async-start | bytes 1572864 | tf_op jit(solution)/shard_map/psum | solution.py:11
  78.5 88.9 %all-gather.11.cloned.1.call-start = ((), (), s32[]{:S(2)}) async-start(), calls=%async_computation.8 | async-start | bytes 3538944 | tf_op jit(solution)/shard_map/all_gather | solution.py:25
  79.5 152.9 %reduce-scatter.5.cloned.1.call-start = ((), (), s32[]{:S(2)}) async-start(), calls=%async_computation.5 | async-start | bytes 1769472 | tf_op jit(solution)/shard_map/reduce_scatter | solution.py:28
  79.5 87.9 %copy-start.1 = (f32[3072,128]{1,0:T(8,128)S(1)}, f32[3072,128]{1,0:T(8,128)}, u32[]{:S(2)}) copy-start(f32[3072,128]{1,0:T(8,128)} %all-gather.7.cloned.1.call-done) | copy-start | bytes 4718596
  168.9 8.0 %copy-start.2 = (f32[1536,128]{1,0:T(8,128)S(1)}, f32[1536,128]{1,0:T(8,128)}, u32[]{:S(2)}) copy-start(f32[1536,128]{1,0:T(8,128)} %all-reduce.3.cloned.1.call-done) | copy-start | bytes 2359300
  199.2 58.5 %all-gather.9.cloned.1.call-start = ((), (), s32[]{:S(2)}) async-start(), calls=%async_computation.6 | async-start | bytes 1769472 | tf_op jit(solution)/shard_map/all_gather | solution.py:36
  232.5 76.1 %all-reduce.5.cloned.1.call-start = ((), (), s32[]{:S(2)}) async-start(), calls=%async_computation.7 | async-start | bytes 1572864 | tf_op jit(solution)/shard_map/psum | solution.py:11
  259.8 89.0 %all-gather.13.cloned.1.call-start = ((), (), s32[]{:S(2)}) async-start(), calls=%async_computation.9 | async-start | bytes 3538944 | tf_op jit(solution)/shard_map/all_gather | solution.py:25
  350.9 8.0 %copy-start.3 = (f32[1536,128]{1,0:T(8,128)S(1)}, f32[1536,128]{1,0:T(8,128)}, u32[]{:S(2)}) copy-start(f32[1536,128]{1,0:T(8,128)} %all-reduce.5.cloned.1.call-done) | copy-start | bytes 2359300
Sparse Core Ops, SparseCore 0:
  14.2 36.8 reduce-scatter.2
  52.8 23.5 all-gather.6
  79.5 47.7 all-reduce.2
  128.8 38.5 all-gather.10
  199.4 33.0 reduce-scatter.4
  233.9 23.7 all-gather.8
  260.7 47.7 all-reduce.4
  310.2 38.6 all-gather.12
where the time goes:
time: 394 us; the launch traced here: 393 us
  waiting for transfers between devices  221 us (56%)
  matrix products  68.3 us (17%)
  blocking collectives  60.1 us (15%)
  local copies, waits for them, and re-layouts  26.3 us (7%)
  between operations  13.6 us (3%)
  other arithmetic  4.14 us (1%)
    psum x2, waiting for transfers between devices, spread(): return lax.psum(block, axis)  82.9 us
    reduce_scatter x2, waiting for transfers between devices, per_device(): lax.psum_scatter(lax.dot_general(tile_now, v_rows, (((0,), (0,)), ((), ()...  70.1 us
    psum x2, blocking collectives, per_device(): lax.psum(local_sum.astype(jnp.bfloat16), 'row').astype(jnp.float32)  60.1 us
    all_gather x2, waiting for transfers between devices, per_device(): av_cols = lax.all_gather(av_fine, 'row', axis=0, tiled=True)  50.3 us
    dot_general x2, matrix products, per_device(): lax.dot_general(w_rows, v_cols, (((1,), (1,)), ((), ())), preferred_eleme...  29.4 us
    all_gather x2, waiting for transfers between devices, per_device(): gathered = lax.all_gather(v_rows, 'row', axis=0, tiled=True)  16.4 us
    dot_general x2, matrix products, per_device(): lax.dot_general(v_rows, w_cols, (((1,), (1,)), ((), ())), preferred_eleme...  16 us
    dot_general x2, matrix products, per_device(): lax.dot_general(tile_now, v_rows, (((0,), (0,)), ((), ())), preferred_ele...  15 us
  transfers between devices with their start and end apart: 8, of which 8 were waited for; matrix products, arithmetic and copies ran while one was open for 4% of the time, Pallas kernels for 0%

commit v1 on v0

--- a/solution.py
+++ b/solution.py
@@ -8,7 +8,7 @@
 
 def spread(block, axis, source):
     block = jnp.where(lax.axis_index(axis) == source, block, jnp.zeros_like(block))
-    return lax.psum(block, axis)
+    return jnp.sum(lax.all_gather(block, axis), axis=0)
 
 
 def per_device(matrix, panels):

time: 394 us -> 382 us (0.970)
  waiting for transfers between devices: 221 us -> 204 us
  other arithmetic: 4.14 us -> 8.69 us
    psum x2 -> x0, waiting for transfers between devices: 82.9 us -> none  [spread(): return lax.psum(block, axis)]
    all_gather x0 -> x2, waiting for transfers between devices: none -> 71.8 us  [spread(): return jnp.sum(lax.all_gather(block, axis), axis=0)]
    all_gather x2, waiting for transfers between devices: 16.4 us -> 10.9 us  [per_device(): gathered = lax.all_gather(v_rows, 'row', axis=0, tiled=True)]
    reduce_sum x0 -> x2, other arithmetic: none -> 4.5 us  [spread(): return jnp.sum(lax.all_gather(block, axis), axis=0)]
    unnamed x9 -> x7, local copies, waits for them, and re-layouts: 12.8 us -> 12.6 us
  transfers between devices with their start and end apart: 8 -> 8, of which waited for: 8 -> 8; matrix products, arithmetic and copies ran while one was open for 4% -> 6% of each run, Pallas kernels for 0% -> 0%
where the time goes in v1:
time: 382 us; the launch traced here: 381 us
  waiting for transfers between devices  204 us (53%)
  matrix products  66.6 us (17%)
  blocking collectives  61.4 us (16%)
  local copies, waits for them, and re-layouts  26.2 us (7%)
  between operations  13.6 us (4%)
  other arithmetic  8.69 us (2%)
    all_gather x2, waiting for transfers between devices, spread(): return jnp.sum(lax.all_gather(block, axis), axis=0)  71.8 us
    reduce_scatter x2, waiting for transfers between devices, per_device(): lax.psum_scatter(lax.dot_general(tile_now, v_rows, (((0,), (0,)), ((), ()...  70.2 us
    psum x2, blocking collectives, per_device(): lax.psum(local_sum.astype(jnp.bfloat16), 'row').astype(jnp.float32)  61.4 us
    all_gather x2, waiting for transfers between devices, per_device(): av_cols = lax.all_gather(av_fine, 'row', axis=0, tiled=True)  50.2 us
    dot_general x2, matrix products, per_device(): lax.dot_general(w_rows, v_cols, (((1,), (1,)), ((), ())), preferred_eleme...  29.3 us
    dot_general x2, matrix products, per_device(): lax.dot_general(v_rows, w_cols, (((1,), (1,)), ((), ())), preferred_eleme...  15.8 us
    dot_general x2, matrix products, per_device(): lax.dot_general(tile_now, v_rows, (((0,), (0,)), ((), ())), preferred_ele...  14.9 us
    convert_element_type x1, local copies, waits for them, and re-layouts, per_device(): a_tile = (a_tile.astype(jnp.float32) - update).astype(jnp.bfloat16)  12.6 us
  transfers between devices with their start and end apart: 8, of which 8 were waited for; matrix products, arithmetic and copies ran while one was open for 6% of the time, Pallas kernels for 0%

profile of v1, /device:TPU:0, one launch (start us, length us, event | category | flops | bytes accessed | tf_op | source)
XLA Modules:
  0.0 380.6 jit_solution(10509218404328819824)
XLA Ops:
  6.5 7.5 %fusion.34 = f32[3072,128]{1,0:T(8,128)} fusion(bf16[1536,3072]{1,0:T(8,128)(2,1)} %param.2, bf16[2,1536,128]{2,1,0:T(8,128)(2,1)} %param.3), kind=kOutput, calls=%fused_computation.44 | convolution fusion | flops 1207959552 | bytes 11403264 | tf_op jit(solution)/shard_map/dot_general | solution.py:29
  14.1 37.0 %reduce-scatter.3.cloned.1.call-done = f32[384,128]{1,0:T(8,128)} async-done(((f32[3072,128]{1,0:T(8,128)}), f32[384,128]{1,0:T(8,128)}) %reduce-scatter.3.cloned.1.call-update) | async-done | bytes 196624 | tf_op jit(solution)/shard_map/reduce_scatter | solution.py:28
  51.2 25.2 %all-gather.11.cloned.1.call-done = f32[3072,128]{1,0:T(8,128)} async-done(((f32[384,128]{1,0:T(8,128)}), f32[3072,128]{1,0:T(8,128)}) %all-gather.11.cloned.1.call-update) | async-done | bytes 1572880 | tf_op jit(solution)/shard_map/all_gather | solution.py:36
  76.3 2.1 dynamic-slice_select_fusion.1
  78.4 0.0 all-gather.15.cloned.1.call-start
  78.5 1.0 fusion.48
  79.5 0.0 reduce-scatter.5.cloned.1.call-start
  79.6 12.6 %copy.3 = bf16[1536,3072]{0,1:T(8,128)(2,1)} copy(bf16[1536,3072]{1,0:T(8,128)(2,1)} %param.2) | data formatting | bytes 18874368 | tf_op args[0]
  92.2 29.4 %all-gather.17.cloned.1.call-done = f32[6144,128]{1,0:T(8,128)} async-done(((f32[1536,128]{1,0:T(8,128)}), f32[6144,128]{1,0:T(8,128)}) %all-gather.17.cloned.1.call-update) | async-done | bytes 3145744 | tf_op jit(solution)/shard_map/all_gather | solution.py:11
  121.6 2.2 reduce_sum.18
  123.8 0.8 fusion.14
  124.6 30.7 %psum.14 = bf16[128,128]{0,1:T(8,128)(2,1)} all-reduce(bf16[128,128]{0,1:T(8,128)(2,1)S(1)} %fusion.14), channel_id=1, replica_groups=mesh['row'=8,'col'=4] {'row'}, use_global_device_ids=true, to_apply=%region_2.3 | all-reduce | flops 16384 | bytes 65536 | tf_op jit(solution)/shard_map/psum | solution.py:40
  155.4 1.0 fusion.13
  156.4 5.4 %all-gather.15.cloned.1.call-done = bf16[1,12288,128]{2,1,0:T(8,128)(2,1)} async-done(((bf16[1,1536,128]{2,1,0:T(8,128)(2,1)}), bf16[1,12288,128]{2,1,0:T(8,128)(2,1)}) %all-gather.15.cloned.1.call-update) | async-done | bytes 3145744 | tf_op jit(solution)/shard_map/all_gather | solution.py:25
  161.8 1.5 fusion.6
  163.3 7.9 %fusion.30 = f32[3072,1536]{1,0:T(8,128)} fusion(bf16[3072,128]{1,0:T(8,128)(2,1)S(1)} %fusion.6, bf16[2,1536,128]{2,1,0:T(8,128)(2,1)S(1)} %copy-done), kind=kOutput, calls=%fused_computation.40 | convolution fusion | flops 1207959552 | bytes 20054016 | tf_op jit(solution)/shard_map/dot_general | solution.py:49
  171.2 14.6 %fusion.3 = bf16[1536,3072]{0,1:T(8,128)(2,1)} fusion(f32[3072,1536]{1,0:T(8,128)} %fusion.30, bf16[1536,3072]{0,1:T(8,128)(2,1)} %copy.3, bf16[1536,128]{1,0:T(8,128)(2,1)S(1)} %fusion.13, bf16[1,12288,128]{2,1,0:T(8,128)(2,1)} %all-gather.15.cloned.1.call-done, s32[]{:T(128)S(6)} %select_n.34), kind=kOutput, calls=%fused_computation.5 | convolution fusion | flops 1226833920 | bytes 38928388 | tf_op jit(solution)/shard_map/dot_general | solution.py:52
  185.7 7.4 %fusion.28 = f32[3072,128]{1,0:T(8,128)} fusion(bf16[1536,3072]{0,1:T(8,128)(2,1)} %fusion.3, bf16[2,1536,128]{2,1,0:T(8,128)(2,1)S(1)} %copy-done), kind=kOutput, calls=%fused_computation.38 | convolution fusion | flops 1207959552 | bytes 11403264 | tf_op jit(solution)/shard_map/dot_general | solution.py:29
  193.3 33.2 %reduce-scatter.5.cloned.1.call-done = f32[384,128]{1,0:T(8,128)} async-done(((f32[3072,128]{1,0:T(8,128)}), f32[384,128]{1,0:T(8,128)}) %reduce-scatter.5.cloned.1.call-update) | async-done | bytes 196624 | tf_op jit(solution)/shard_map/reduce_scatter | solution.py:28
  226.5 25.0 %all-gather.13.cloned.1.call-done = f32[3072,128]{1,0:T(8,128)} async-done(((f32[384,128]{1,0:T(8,128)}), f32[3072,128]{1,0:T(8,128)}) %all-gather.13.cloned.1.call-update) | async-done | bytes 1572880 | tf_op jit(solution)/shard_map/all_gather | solution.py:36
  251.5 2.1 dynamic-slice_select_fusion
  253.7 0.7 all-gather.19.cloned.1.call-update
  254.4 42.4 %all-gather.21.cloned.1.call-done = f32[6144,128]{1,0:T(8,128)} async-done(((f32[1536,128]{1,0:T(8,128)}), f32[6144,128]{1,0:T(8,128)}) %all-gather.21.cloned.1.call-update) | async-done | bytes 3145744 | tf_op jit(solution)/shard_map/all_gather | solution.py:11
  296.8 2.2 reduce_sum.19
  299.0 0.8 fusion.15
  299.8 30.7 %psum.15 = bf16[128,128]{0,1:T(8,128)(2,1)} all-reduce(bf16[128,128]{0,1:T(8,128)(2,1)S(1)} %fusion.15), channel_id=1, replica_groups=mesh['row'=8,'col'=4] {'row'}, use_global_device_ids=true, to_apply=%region_5.6 | all-reduce | flops 16384 | bytes 65536 | tf_op jit(solution)/shard_map/psum | solution.py:40
  330.5 1.0 fusion.12
  331.6 5.5 %all-gather.19.cloned.1.call-done = bf16[1,12288,128]{2,1,0:T(8,128)(2,1)} async-done(((bf16[1,1536,128]{2,1,0:T(8,128)(2,1)}), bf16[1,12288,128]{2,1,0:T(8,128)(2,1)}) %all-gather.19.cloned.1.call-update) | async-done | bytes 3145744 | tf_op jit(solution)/shard_map/all_gather | solution.py:25
  337.1 1.5 fusion.7
  338.6 7.9 %fusion.24 = f32[3072,1536]{1,0:T(8,128)} fusion(bf16[3072,128]{1,0:T(8,128)(2,1)S(1)} %fusion.7, bf16[2,1536,128]{2,1,0:T(8,128)(2,1)S(1)} %copy-done), kind=kOutput, calls=%fused_computation.34 | convolution fusion | flops 1207959552 | bytes 20054016 | tf_op jit(solution)/shard_map/dot_general | solution.py:49
  346.5 14.7 %fusion.1 = bf16[1536,3072]{0,1:T(8,128)(2,1)} fusion(f32[3072,1536]{1,0:T(8,128)} %fusion.24, bf16[1536,3072]{0,1:T(8,128)(2,1)} %fusion.3, bf16[1536,128]{1,0:T(8,128)(2,1)S(1)} %fusion.12, bf16[1,12288,128]{2,1,0:T(8,128)(2,1)} %all-gather.19.cloned.1.call-done, s32[]{:T(128)S(6)} %select_n.34), kind=kOutput, calls=%fused_computation.2 | convolution fusion | flops 1226833920 | bytes 38928388 | tf_op jit(solution)/shard_map/dot_general | solution.py:52
  361.2 12.6 %copy.6 = bf16[1536,3072]{1,0:T(8,128)(2,1)} copy(bf16[1536,3072]{0,1:T(8,128)(2,1)} %fusion.1) | data formatting | bytes 18874368 | tf_op jit(solution)/shard_map/convert_element_type | solution.py:55
  (19 shorter events, 0.3 us)
Async XLA Ops:
  6.5 44.5 %reduce-scatter.3.cloned.1.call-start = ((), (), s32[]{:S(2)}) async-start(), calls=%async_computation.2 | async-start | bytes 1769472 | tf_op jit(solution)/shard_map/reduce_scatter | solution.py:28
  14.0 64.5 %copy-start = (bf16[2,1536,128]{2,1,0:T(8,128)(2,1)S(1)}, bf16[2,1536,128]{2,1,0:T(8,128)(2,1)}, u32[]{:S(2)}) copy-start(bf16[2,1536,128]{2,1,0:T(8,128)(2,1)} %param.3) | copy-start | bytes 2359300
  14.0 62.3 %all-gather.11.cloned.1.call-start = ((), (), s32[]{:S(2)}) async-start(), calls=%async_computation.3 | async-start | bytes 1769472 | tf_op jit(solution)/shard_map/all_gather | solution.py:36
  51.1 70.5 %all-gather.17.cloned.1.call-start = ((), (), s32[]{:S(2)}) async-start(), calls=%async_computation.7 | async-start | bytes 3932160 | tf_op jit(solution)/shard_map/all_gather | solution.py:11
  78.4 83.3 %all-gather.15.cloned.1.call-start = ((), (), s32[]{:S(2)}) async-start(), calls=%async_computation.6 | async-start | bytes 3538944 | tf_op jit(solution)/shard_map/all_gather | solution.py:25
  79.5 146.9 %reduce-scatter.5.cloned.1.call-start = ((), (), s32[]{:S(2)}) async-start(), calls=%async_computation.4 | async-start | bytes 1769472 | tf_op jit(solution)/shard_map/reduce_scatter | solution.py:28
  121.6 40.2 %copy-start.1 = (f32[3072,128]{1,0:T(8,128)S(1)}, f32[3072,128]{1,0:T(8,128)}, u32[]{:S(2)}) copy-start(f32[3072,128]{1,0:T(8,128)} %all-gather.11.cloned.1.call-done) | copy-start | bytes 4718596
  193.2 58.3 %all-gather.13.cloned.1.call-start = ((), (), s32[]{:S(2)}) async-start(), calls=%async_computation.5 | async-start | bytes 1769472 | tf_op jit(solution)/shard_map/all_gather | solution.py:36
  226.5 70.3 %all-gather.21.cloned.1.call-start = ((), (), s32[]{:S(2)}) async-start(), calls=%async_computation.9 | async-start | bytes 3932160 | tf_op jit(solution)/shard_map/all_gather | solution.py:11
  253.6 83.4 %all-gather.19.cloned.1.call-start = ((), (), s32[]{:S(2)}) async-start(), calls=%async_computation.8 | async-start | bytes 3538944 | tf_op jit(solution)/shard_map/all_gather | solution.py:25
  296.8 40.3 %copy-start.2 = (f32[3072,128]{1,0:T(8,128)S(1)}, f32[3072,128]{1,0:T(8,128)}, u32[]{:S(2)}) copy-start(f32[3072,128]{1,0:T(8,128)} %all-gather.13.cloned.1.call-done) | copy-start | bytes 4718596
Sparse Core Ops, SparseCore 0:
  14.2 36.8 reduce-scatter.2
  52.7 23.5 all-gather.10
  78.6 42.9 all-gather.16
  123.1 38.6 all-gather.14
  193.3 33.0 reduce-scatter.4
  227.9 23.5 all-gather.12
  253.8 42.9 all-gather.20
  298.4 38.6 all-gather.18
